TPU v7x, 32 devices: a whole 2x2x4 slice. The times are simulated.
32 devices in a mesh: blk: 8 (over z, core), uly: 4 (over y, x).
Axes of the slice: x: 2, y: 2, z: 4, core: 2. Of those that a mesh axis runs over, the one named last changes fastest.
Arguments:
- queries: bfloat16 [1024, 128, 128], P(('blk', 'uly')), may hold values from -8 to 8
- query_tangents: bfloat16 [1024, 128, 4, 128], P(('blk', 'uly')), may hold values from -6 to 6
- keys: bfloat16 [1024, 8, 128], P(('blk', 'uly')), may hold values from -8 to 8
- key_tangents: bfloat16 [1024, 8, 4, 128], P(('blk', 'uly')), may hold values from -6 to 6
- values: bfloat16 [1024, 8, 128], P(('blk', 'uly')), may hold values from -6 to 6
- value_tangents: bfloat16 [1024, 8, 4, 128], P(('blk', 'uly')), may hold values from -6 to 6
- span_order: int32 [16], replicated, may hold values from 0 to 15, as said below
Outputs:
- attention_out: bfloat16 [1024, 128, 128], P(('blk', 'uly'))
- tangent_out: bfloat16 [1024, 128, 4, 128], P(('blk', 'uly'))
Inputs may be any that keep to these rules, and one draw needn't show every extreme that they name: span_order is a permutation of the span positions; for every b the stored spans 2 * b and 2 * b + 1 hold positions c and 15 - c for some c.
All inputs are finite; a program needn't handle non-finite values.
Results may differ from a plain program's by a relative error of at most 0.0055.
Values may be sent and summed in bfloat16 or wider, within the bound.
A program may use at most 128 MiB of HBM per device.

v0:
```python
import jax
import jax.numpy as jnp
from jax import lax
from jax.sharding import PartitionSpec as P

HQ = 128
KVH = 8


def positions(stored, span_order, span_rows):
    span_ids = stored // span_rows
    table_ids = jnp.arange(span_order.shape[0], dtype=jnp.int32)
    looked_up = jnp.sum(
        jnp.where(span_ids[:, None] == table_ids[None, :], span_order[None, :], 0), axis=1
    )
    return looked_up * span_rows + stored % span_rows


def per_device(queries, query_tangents, keys, key_tangents, values, value_tangents, span_order):
    local_queries, local_tangents = (
        lax.all_to_all(queries, "uly", split_axis=1, concat_axis=0, tiled=True),
        lax.all_to_all(query_tangents, "uly", split_axis=1, concat_axis=0, tiled=True),
    )
    query_rows = local_queries.shape[0]
    span_rows = query_rows // 2
    head_size = local_queries.shape[2]
    group = HQ // KVH
    kv_local = local_queries.shape[1] // group
    probes = local_tangents.shape[2]
    scaling = head_size ** (-0.5)
    stored = lax.axis_index("blk") * query_rows + jnp.arange(query_rows, dtype=jnp.int32)
    query_places = positions(stored, span_order, span_rows)
    latest = jnp.max(query_places)
    query_heads = jnp.transpose(
        local_queries.reshape(query_rows, kv_local, group, head_size), (1, 2, 0, 3)
    )
    tangent_heads = jnp.transpose(
        local_tangents.reshape(query_rows, kv_local, group, probes, head_size), (1, 2, 3, 0, 4)
    )

    def update(carry, block):
        key_block, key_tan, value_block, value_tan, key_places = block
        running_max, totals, primal_sums, tangent_sums, shifts = carry
        visible = key_places[None, :] <= query_places[:, None]
        scores = (
            jnp.einsum("grqd,kgd->grqk", query_heads, key_block, preferred_element_type=jnp.float32)
            * scaling
        )
        scores = jnp.where(visible[None, None], scores, -1e30)
        new_max = jnp.maximum(running_max, jnp.max(scores, axis=-1))
        rescale = jnp.exp(running_max - new_max)
        weights_full = jnp.where(visible[None, None], jnp.exp(scores - new_max[..., None]), 0.0)
        weights_half = weights_full.astype(jnp.bfloat16)
        score_tan = jnp.einsum(
            "grpqd,kgd->grpqk", tangent_heads, key_block, preferred_element_type=jnp.float32
        )
        score_tan = score_tan + jnp.einsum(
            "grqd,kgpd->grpqk", query_heads, key_tan, preferred_element_type=jnp.float32
        )
        weighted = weights_full[:, :, None] * (score_tan * scaling)
        totals = totals * rescale + jnp.sum(weights_full, axis=-1)
        primal_sums = primal_sums * rescale[..., None] + jnp.einsum(
            "grqk,kgd->grqd", weights_half, value_block, preferred_element_type=jnp.float32
        )
        shifts = shifts * rescale[:, :, None] + jnp.sum(weighted, axis=-1)
        tangent_sums = tangent_sums * rescale[:, :, None, :, None]
        tangent_sums = tangent_sums + jnp.einsum(
            "grpqk,kgd->grpqd",
            weighted.astype(jnp.bfloat16),
            value_block,
            preferred_element_type=jnp.float32,
        )
        tangent_sums = tangent_sums + jnp.einsum(
            "grqk,kgpd->grpqd", weights_half, value_tan, preferred_element_type=jnp.float32
        )
        return (new_max, totals, primal_sums, tangent_sums, shifts)

    def keep_state(carry, block):
        return carry

    def visit(carry, block):
        reachable = jnp.min(block[4]) <= latest
        return (lax.cond(reachable, update, keep_state, carry, block), None)

    initial = (
        jnp.full((kv_local, group, query_rows), -1e30, jnp.float32),
        jnp.zeros((kv_local, group, query_rows), jnp.float32),
        jnp.zeros((kv_local, group, query_rows, head_size), jnp.float32),
        jnp.zeros((kv_local, group, probes, query_rows, head_size), jnp.float32),
        jnp.zeros((kv_local, group, probes, query_rows), jnp.float32),
    )
    head_keys, head_key_tan, head_values, head_value_tan = (
        lax.all_to_all(keys, "uly", split_axis=1, concat_axis=0, tiled=True),
        lax.all_to_all(key_tangents, "uly", split_axis=1, concat_axis=0, tiled=True),
        lax.all_to_all(values, "uly", split_axis=1, concat_axis=0, tiled=True),
        lax.all_to_all(value_tangents, "uly", split_axis=1, concat_axis=0, tiled=True),
    )
    carry = initial
    key_piece = lax.all_gather(head_keys, "blk", axis=0, tiled=True)
    key_tan_piece = lax.all_gather(head_key_tan, "blk", axis=0, tiled=True)
    value_piece = lax.all_gather(head_values, "blk", axis=0, tiled=True)
    value_tan_piece = lax.all_gather(head_value_tan, "blk", axis=0, tiled=True)
    piece_rows = key_piece.shape[0]
    block_rows = 256
    block_total = piece_rows // block_rows
    places = positions(jnp.arange(piece_rows, dtype=jnp.int32), span_order, span_rows)
    stacked = (
        key_piece.reshape(block_total, block_rows, kv_local, head_size),
        key_tan_piece.reshape(block_total, block_rows, kv_local, probes, head_size),
        value_piece.reshape(block_total, block_rows, kv_local, head_size),
        value_tan_piece.reshape(block_total, block_rows, kv_local, probes, head_size),
        places.reshape(block_total, block_rows),
    )
    carry, unused = lax.scan(visit, carry, stacked)
    running_max, totals, primal_sums, tangent_sums, shifts = carry
    primal = primal_sums / totals[..., None]
    tangent = (
        tangent_sums / totals[:, :, None, :, None]
        - primal[:, :, None] * (shifts / totals[:, :, None])[..., None]
    )
    output_rows = jnp.transpose(primal.astype(jnp.bfloat16), (2, 0, 1, 3)).reshape(
        query_rows, kv_local * group, head_size
    )
    tangent_rows = jnp.transpose(tangent.astype(jnp.bfloat16), (3, 0, 1, 2, 4)).reshape(
        query_rows, kv_local * group, probes, head_size
    )
    attention_out, tangent_out = (
        lax.all_to_all(output_rows, "uly", split_axis=0, concat_axis=1, tiled=True),
        lax.all_to_all(tangent_rows, "uly", split_axis=0, concat_axis=1, tiled=True),
    )
    return (attention_out, tangent_out)


def solution(mesh):
    placed = (
        P(("blk", "uly"), None, None),
        P(("blk", "uly"), None, None, None),
        P(("blk", "uly"), None, None),
        P(("blk", "uly"), None, None, None),
        P(("blk", "uly"), None, None),
        P(("blk", "uly"), None, None, None),
        P(),
    )
    return jax.shard_map(
        per_device,
        mesh=mesh,
        in_specs=placed,
        out_specs=(P(("blk", "uly"), None, None), P(("blk", "uly"), None, None, None)),
        check_vma=False,
    )
```

profile of v0, /device:TPU:0, one launch (start us, length us, event | category | flops | bytes accessed | tf_op | source)
XLA Modules:
  0.0 424.2 jit_solution(10656126634466372391)
XLA Ops:
  8.3 10.7 %all_to_all.138 = bf16[32,8,4,128]{3,0,2,1:T(8,128)(2,1)S(1)} all-to-all(bf16[32,8,4,128]{3,0,2,1:T(8,128)(2,1)S(1)} %copy.84), channel_id=1, replica_groups=mesh['blk'=8,'uly'=4] {'uly'}, dimensions={1} | all-to-all | bytes 524288 | tf_op jit(solution)/shard_map/all_to_all | solution.py:94
  65.5 17.9 %all_gather.12 = bf16[1024,2,128]{2,0,1:T(8,128)(2,1)S(1)} all-gather(bf16[128,2,128]{2,0,1:T(8,128)(2,1)S(1)} %bitcast.140), channel_id=1, replica_groups=mesh['blk'=8,'uly'=4] {'blk'}, dimensions={0}, use_global_device_ids=true | all-gather | bytes 589824 | tf_op jit(solution)/shard_map/all_gather | solution.py:99
  84.2 14.7 %all_gather.13 = bf16[1024,2,128]{2,0,1:T(8,128)(2,1)S(1)} all-gather(bf16[128,2,128]{2,0,1:T(8,128)(2,1)S(1)} %bitcast.141), channel_id=1, replica_groups=mesh['blk'=8,'uly'=4] {'blk'}, dimensions={0}, use_global_device_ids=true | all-gather | bytes 589824 | tf_op jit(solution)/shard_map/all_gather | solution.py:101
  123.5 212.6 %while.18 = (s32[]{:T(128)}, f32[2,16,128]{2,1,0:T(8,128)S(1)}, f32[2,16,128]{2,1,0:T(8,128)S(1)}, f32[2,16,128,128]{3,2,1,0:T(8,128)}, f32[2,16,4,128,128]{4,3,...) while((s32[]{:T(128)}, f32[2,16,128]{2,1,0:T(8,128)S(1)}, ...), condition=%wide.region_10.11_spmd, body=%wide.region_3.10_spmd.sunk | while | flops 4875936256 | bytes 138631600 | solution.py:114
  125.7 51.1 %conditional.2 = ((f32[2,16,128]{2,1,0:T(8,128)S(1)}, f32[2,16,128]{2,1,0:T(8,128)S(1)}, f32[2,16,128,128]{3,2,1,0:T(8,128)}, f32[2,16,4,128,128]{4,3,2,1,0:T(8,128)}, f32[2,16,4,128]{3,2,1,0:T(4,128)S(1)})) conditional(s32[]{:T(128)} %convert_element_type.33, (f32[2,16,128]{2,1,0:T(8,128)S(1)}, f32[2,16,128]{2,1,0:T(8,128)S(1)}, ...), branch_computations={%region_5.5_spmd, %region_6.9_spmd} | conditional | flops 4875935744 | bytes 138629216 | solution.py:83
  130.8 9.1 %fusion.7 = f32[2,256,4,16,128]{4,1,2,3,0:T(8,128)} fusion(bf16[2,16,128,128]{3,2,1,0:T(8,128)(2,1)S(1)} %get-tuple-element.183, bf16[4,256,2,4,128]{4,1,3,2,0:T(8,128)(2,1)} %get-tuple-element.189, s32[]{:T(128)} %get-tuple-element.182), kind=kOutput, calls=%fused_computation.13 | convolution fusion | flops 1073741824 | bytes 18350592 | tf_op jit(solution)/shard_map/while/body/eval_jaxpr/cond/branch_1_fun/grqd,kgpd->grpqk/dot_general | solution.py:57
  139.9 13.2 %fusion.40 = (f32[2,16,4,128]{3,2,1,0:T(4,128)S(1)}, bf16[2,16,4,128,256]{3,4,2,1,0:T(8,128)(2,1)}) fusion(f32[2,16,128,256]{2,3,1,0:T(8,128)} %get-tuple-element.327, f32[2,256,4,16,128]{4,1,2,3,0:T(8,128)} %fusion.7, bf16[2,16,4,128,128]{4,3,2,1,0:T(8,128)(2,1)} %get-tuple-element.188, bf16[4,256,2,128]{3,1,2,0:T(8,128)(2,1)} %get-tuple-element.181, ...), kind=kOutput, calls=%fused_computation.70 | convolution fusion | flops 1090502656 | bytes 33751552 | tf_op jit(solution)/shard_map/while/body/eval_jaxpr/cond/branch_1_fun/grpqd,kgd->grpqk/dot_general | solution.py:54
  153.1 10.0 %fusion.1 = f32[2,16,4,128,128]{4,3,2,1,0:T(8,128)} fusion(bf16[2,16,4,128,256]{3,4,2,1,0:T(8,128)(2,1)} %get-tuple-element.332, bf16[4,256,2,128]{3,1,2,0:T(8,128)(2,1)} %get-tuple-element.186, s32[]{:T(128)} %get-tuple-element.182), kind=kOutput, calls=%fused_computation.3 | convolution fusion | flops 1073741824 | bytes 16908800 | tf_op jit(solution)/shard_map/while/body/eval_jaxpr/cond/branch_1_fun/grpqk,kgd->grpqd/dot_general | solution.py:67
  163.2 9.5 %bitcast_add_fusion.1 = f32[2,16,4,128,128]{4,3,2,1,0:T(8,128)} fusion(f32[2,16,4,128,128]{4,3,2,1,0:T(8,128)} %fusion.1, f32[2,16,4,128,128]{4,3,2,1,0:T(8,128)} %get-tuple-element.187, f32[2,16,128]{2,1,0:T(8,128)S(1)} %get-tuple-element.320, bf16[4,256,2,4,128]{4,1,3,2,0:T(8,128)(2,1)S(1)} %get-tuple-element.190, s32[]{:T(128)} %get-tuple-element.182, ...), kind=kOutput, calls=%fused_computation.2 | convolution fusion | flops 1085276160 | bytes 29949956 | tf_op jit(solution)/shard_map/while/body/eval_jaxpr/cond/branch_1_fun/grqk,kgpd->grpqd/dot_general | solution.py:73
  178.8 51.1 %conditional.2 = ((f32[2,16,128]{2,1,0:T(8,128)S(1)}, f32[2,16,128]{2,1,0:T(8,128)S(1)}, f32[2,16,128,128]{3,2,1,0:T(8,128)}, f32[2,16,4,128,128]{4,3,2,1,0:T(8,128)}, f32[2,16,4,128]{3,2,1,0:T(4,128)S(1)})) conditional(s32[]{:T(128)} %convert_element_type.33, (f32[2,16,128]{2,1,0:T(8,128)S(1)}, f32[2,16,128]{2,1,0:T(8,128)S(1)}, ...), branch_computations={%region_5.5_spmd, %region_6.9_spmd} | conditional | flops 4875935744 | bytes 138629216 | solution.py:83
  183.9 9.1 %fusion.7 = f32[2,256,4,16,128]{4,1,2,3,0:T(8,128)} fusion(bf16[2,16,128,128]{3,2,1,0:T(8,128)(2,1)S(1)} %get-tuple-element.183, bf16[4,256,2,4,128]{4,1,3,2,0:T(8,128)(2,1)} %get-tuple-element.189, s32[]{:T(128)} %get-tuple-element.182), kind=kOutput, calls=%fused_computation.13 | convolution fusion | flops 1073741824 | bytes 18350592 | tf_op jit(solution)/shard_map/while/body/eval_jaxpr/cond/branch_1_fun/grqd,kgpd->grpqk/dot_general | solution.py:57
  193.0 13.2 %fusion.40 = (f32[2,16,4,128]{3,2,1,0:T(4,128)S(1)}, bf16[2,16,4,128,256]{3,4,2,1,0:T(8,128)(2,1)}) fusion(f32[2,16,128,256]{2,3,1,0:T(8,128)} %get-tuple-element.327, f32[2,256,4,16,128]{4,1,2,3,0:T(8,128)} %fusion.7, bf16[2,16,4,128,128]{4,3,2,1,0:T(8,128)(2,1)} %get-tuple-element.188, bf16[4,256,2,128]{3,1,2,0:T(8,128)(2,1)} %get-tuple-element.181, ...), kind=kOutput, calls=%fused_computation.70 | convolution fusion | flops 1090502656 | bytes 33751552 | tf_op jit(solution)/shard_map/while/body/eval_jaxpr/cond/branch_1_fun/grpqd,kgd->grpqk/dot_general | solution.py:54
  206.3 10.0 %fusion.1 = f32[2,16,4,128,128]{4,3,2,1,0:T(8,128)} fusion(bf16[2,16,4,128,256]{3,4,2,1,0:T(8,128)(2,1)} %get-tuple-element.332, bf16[4,256,2,128]{3,1,2,0:T(8,128)(2,1)} %get-tuple-element.186, s32[]{:T(128)} %get-tuple-element.182), kind=kOutput, calls=%fused_computation.3 | convolution fusion | flops 1073741824 | bytes 16908800 | tf_op jit(solution)/shard_map/while/body/eval_jaxpr/cond/branch_1_fun/grpqk,kgd->grpqd/dot_general | solution.py:67
  216.3 9.5 %bitcast_add_fusion.1 = f32[2,16,4,128,128]{4,3,2,1,0:T(8,128)} fusion(f32[2,16,4,128,128]{4,3,2,1,0:T(8,128)} %fusion.1, f32[2,16,4,128,128]{4,3,2,1,0:T(8,128)} %get-tuple-element.187, f32[2,16,128]{2,1,0:T(8,128)S(1)} %get-tuple-element.320, bf16[4,256,2,4,128]{4,1,3,2,0:T(8,128)(2,1)S(1)} %get-tuple-element.190, s32[]{:T(128)} %get-tuple-element.182, ...), kind=kOutput, calls=%fused_computation.2 | convolution fusion | flops 1085276160 | bytes 29949956 | tf_op jit(solution)/shard_map/while/body/eval_jaxpr/cond/branch_1_fun/grqk,kgpd->grpqd/dot_general | solution.py:73
  231.9 51.1 %conditional.2 = ((f32[2,16,128]{2,1,0:T(8,128)S(1)}, f32[2,16,128]{2,1,0:T(8,128)S(1)}, f32[2,16,128,128]{3,2,1,0:T(8,128)}, f32[2,16,4,128,128]{4,3,2,1,0:T(8,128)}, f32[2,16,4,128]{3,2,1,0:T(4,128)S(1)})) conditional(s32[]{:T(128)} %convert_element_type.33, (f32[2,16,128]{2,1,0:T(8,128)S(1)}, f32[2,16,128]{2,1,0:T(8,128)S(1)}, ...), branch_computations={%region_5.5_spmd, %region_6.9_spmd} | conditional | flops 4875935744 | bytes 138629216 | solution.py:83
  237.0 9.1 %fusion.7 = f32[2,256,4,16,128]{4,1,2,3,0:T(8,128)} fusion(bf16[2,16,128,128]{3,2,1,0:T(8,128)(2,1)S(1)} %get-tuple-element.183, bf16[4,256,2,4,128]{4,1,3,2,0:T(8,128)(2,1)} %get-tuple-element.189, s32[]{:T(128)} %get-tuple-element.182), kind=kOutput, calls=%fused_computation.13 | convolution fusion | flops 1073741824 | bytes 18350592 | tf_op jit(solution)/shard_map/while/body/eval_jaxpr/cond/branch_1_fun/grqd,kgpd->grpqk/dot_general | solution.py:57
  246.1 13.2 %fusion.40 = (f32[2,16,4,128]{3,2,1,0:T(4,128)S(1)}, bf16[2,16,4,128,256]{3,4,2,1,0:T(8,128)(2,1)}) fusion(f32[2,16,128,256]{2,3,1,0:T(8,128)} %get-tuple-element.327, f32[2,256,4,16,128]{4,1,2,3,0:T(8,128)} %fusion.7, bf16[2,16,4,128,128]{4,3,2,1,0:T(8,128)(2,1)} %get-tuple-element.188, bf16[4,256,2,128]{3,1,2,0:T(8,128)(2,1)} %get-tuple-element.181, ...), kind=kOutput, calls=%fused_computation.70 | convolution fusion | flops 1090502656 | bytes 33751552 | tf_op jit(solution)/shard_map/while/body/eval_jaxpr/cond/branch_1_fun/grpqd,kgd->grpqk/dot_general | solution.py:54
  259.4 10.0 %fusion.1 = f32[2,16,4,128,128]{4,3,2,1,0:T(8,128)} fusion(bf16[2,16,4,128,256]{3,4,2,1,0:T(8,128)(2,1)} %get-tuple-element.332, bf16[4,256,2,128]{3,1,2,0:T(8,128)(2,1)} %get-tuple-element.186, s32[]{:T(128)} %get-tuple-element.182), kind=kOutput, calls=%fused_computation.3 | convolution fusion | flops 1073741824 | bytes 16908800 | tf_op jit(solution)/shard_map/while/body/eval_jaxpr/cond/branch_1_fun/grpqk,kgd->grpqd/dot_general | solution.py:67
  269.4 9.5 %bitcast_add_fusion.1 = f32[2,16,4,128,128]{4,3,2,1,0:T(8,128)} fusion(f32[2,16,4,128,128]{4,3,2,1,0:T(8,128)} %fusion.1, f32[2,16,4,128,128]{4,3,2,1,0:T(8,128)} %get-tuple-element.187, f32[2,16,128]{2,1,0:T(8,128)S(1)} %get-tuple-element.320, bf16[4,256,2,4,128]{4,1,3,2,0:T(8,128)(2,1)S(1)} %get-tuple-element.190, s32[]{:T(128)} %get-tuple-element.182, ...), kind=kOutput, calls=%fused_computation.2 | convolution fusion | flops 1085276160 | bytes 29949956 | tf_op jit(solution)/shard_map/while/body/eval_jaxpr/cond/branch_1_fun/grqk,kgpd->grpqd/dot_general | solution.py:73
  285.0 51.1 %conditional.2 = ((f32[2,16,128]{2,1,0:T(8,128)S(1)}, f32[2,16,128]{2,1,0:T(8,128)S(1)}, f32[2,16,128,128]{3,2,1,0:T(8,128)}, f32[2,16,4,128,128]{4,3,2,1,0:T(8,128)}, f32[2,16,4,128]{3,2,1,0:T(4,128)S(1)})) conditional(s32[]{:T(128)} %convert_element_type.33, (f32[2,16,128]{2,1,0:T(8,128)S(1)}, f32[2,16,128]{2,1,0:T(8,128)S(1)}, ...), branch_computations={%region_5.5_spmd, %region_6.9_spmd} | conditional | flops 4875935744 | bytes 138629216 | solution.py:83
  299.2 13.2 %fusion.40 = (f32[2,16,4,128]{3,2,1,0:T(4,128)S(1)}, bf16[2,16,4,128,256]{3,4,2,1,0:T(8,128)(2,1)}) fusion(f32[2,16,128,256]{2,3,1,0:T(8,128)} %get-tuple-element.327, f32[2,256,4,16,128]{4,1,2,3,0:T(8,128)} %fusion.7, bf16[2,16,4,128,128]{4,3,2,1,0:T(8,128)(2,1)} %get-tuple-element.188, bf16[4,256,2,128]{3,1,2,0:T(8,128)(2,1)} %get-tuple-element.181, ...), kind=kOutput, calls=%fused_computation.70 | convolution fusion | flops 1090502656 | bytes 33751552 | tf_op jit(solution)/shard_map/while/body/eval_jaxpr/cond/branch_1_fun/grpqd,kgd->grpqk/dot_general | solution.py:54
  312.5 10.0 %fusion.1 = f32[2,16,4,128,128]{4,3,2,1,0:T(8,128)} fusion(bf16[2,16,4,128,256]{3,4,2,1,0:T(8,128)(2,1)} %get-tuple-element.332, bf16[4,256,2,128]{3,1,2,0:T(8,128)(2,1)} %get-tuple-element.186, s32[]{:T(128)} %get-tuple-element.182), kind=kOutput, calls=%fused_computation.3 | convolution fusion | flops 1073741824 | bytes 16908800 | tf_op jit(solution)/shard_map/while/body/eval_jaxpr/cond/branch_1_fun/grpqk,kgd->grpqd/dot_general | solution.py:67
  322.5 9.5 %bitcast_add_fusion.1 = f32[2,16,4,128,128]{4,3,2,1,0:T(8,128)} fusion(f32[2,16,4,128,128]{4,3,2,1,0:T(8,128)} %fusion.1, f32[2,16,4,128,128]{4,3,2,1,0:T(8,128)} %get-tuple-element.187, f32[2,16,128]{2,1,0:T(8,128)S(1)} %get-tuple-element.320, bf16[4,256,2,4,128]{4,1,3,2,0:T(8,128)(2,1)S(1)} %get-tuple-element.190, s32[]{:T(128)} %get-tuple-element.182, ...), kind=kOutput, calls=%fused_computation.2 | convolution fusion | flops 1085276160 | bytes 29949956 | tf_op jit(solution)/shard_map/while/body/eval_jaxpr/cond/branch_1_fun/grqk,kgpd->grpqd/dot_general | solution.py:73
  362.4 45.8 %all-to-all-done.7 = bf16[128,32,4,128]{3,1,2,0:T(8,128)(2,1)} async-done(((bf16[128,32,4,128]{3,1,2,0:T(8,128)(2,1)}), bf16[128,32,4,128]{3,1,2,0:T(8,128)(2,1)}, u32[]{:S(2)}, u32[]{:S(2)}) %all-to-all-start.7) | async-done | bytes 4194336 | tf_op jit(solution)/shard_map/all_to_all | solution.py:129
  (111 shorter events, 156.9 us)
Async XLA Ops:
  7.2 105.6 %all-gather.3.cloned.1.call-start = ((), (), s32[]{:S(2)}) async-start(), calls=%async_computation.8 | async-start | bytes 2359296 | tf_op jit(solution)/shard_map/all_gather | solution.py:100
  21.2 8.1 %all-to-all-start = ((bf16[32,8,128]{2,0,1:T(8,128)(2,1)}), bf16[32,8,128]{2,0,1:T(8,128)(2,1)S(1)}, u32[]{:S(2)}, u32[]{:S(2)}) async-start(bf16[32,8,128]{2,0,1:T(8,128)(2,1)} %copy.76), calls=%async_computation | async-start | bytes 131072 | tf_op jit(solution)/shard_map/all_to_all | solution.py:93
  29.3 8.1 %all-to-all-start.2 = ((bf16[32,8,128]{2,0,1:T(8,128)(2,1)}), bf16[32,8,128]{2,0,1:T(8,128)(2,1)S(1)}, u32[]{:S(2)}, u32[]{:S(2)}) async-start(bf16[32,8,128]{2,0,1:T(8,128)(2,1)} %copy.80), calls=%async_computation.2 | async-start | bytes 131072 | tf_op jit(solution)/shard_map/all_to_all | solution.py:95
  37.4 8.8 %all-to-all-start.5 = ((bf16[32,8,4,128]{3,0,2,1:T(8,128)(2,1)}), bf16[32,8,4,128]{3,0,2,1:T(8,128)(2,1)S(1)}, u32[]{:S(2)}, u32[]{:S(2)}) async-start(bf16[32,8,4,128]{3,0,2,1:T(8,128)(2,1)} %copy.86), calls=%async_computation.5 | async-start | bytes 524288 | tf_op jit(solution)/shard_map/all_to_all | solution.py:96
  46.2 13.5 %all-to-all-start.1 = ((bf16[32,128,128]{2,0,1:T(8,128)(2,1)}), bf16[32,128,128]{2,0,1:T(8,128)(2,1)S(1)}, u32[]{:S(2)}, u32[]{:S(2)}) async-start(bf16[32,128,128]{2,0,1:T(8,128)(2,1)} %copy.78), calls=%async_computation.1 | async-start | bytes 2097152 | tf_op jit(solution)/shard_map/all_to_all | solution.py:21
  49.7 66.2 %all-gather.5.cloned.1.call-start = ((), (), s32[]{:S(2)}) async-start(), calls=%async_computation.9 | async-start | bytes 2359296 | tf_op jit(solution)/shard_map/all_gather | solution.py:102
  57.1 7.4 %copy-start.2 = (s32[16]{0:T(128)S(1)}, s32[16]{0:T(128)}, u32[]{:S(2)}) copy-start(s32[16]{0:T(128)} %param.17) | copy-start | bytes 196
  59.7 47.7 %all-to-all-start.3 = ((bf16[32,128,4,128]{3,2,0,1:T(4,128)(2,1)}), bf16[32,128,4,128]{3,2,0,1:T(4,128)(2,1)}, u32[]{:S(2)}, u32[]{:S(2)}) async-start(bf16[32,128,4,128]{3,2,0,1:T(4,128)(2,1)} %copy.82), calls=%async_computation.3 | async-start | bytes 8388608 | tf_op jit(solution)/shard_map/all_to_all | solution.py:22
  163.1 9.6 %copy-start = (f32[2,16,128,128]{3,2,1,0:T(8,128)S(1)}, f32[2,16,128,128]{3,2,1,0:T(8,128)}, u32[]{:S(2)}) copy-start(f32[2,16,128,128]{3,2,1,0:T(8,128)} %get-tuple-element.185) | copy-start | bytes 6291460 | tf_op jit(solution)/shard_map/while/body/eval_jaxpr/cond
  175.5 1.3 copy-start.1
  216.2 9.6 %copy-start = (f32[2,16,128,128]{3,2,1,0:T(8,128)S(1)}, f32[2,16,128,128]{3,2,1,0:T(8,128)}, u32[]{:S(2)}) copy-start(f32[2,16,128,128]{3,2,1,0:T(8,128)} %get-tuple-element.185) | copy-start | bytes 6291460 | tf_op jit(solution)/shard_map/while/body/eval_jaxpr/cond
  228.6 1.3 copy-start.1
  269.4 9.6 %copy-start = (f32[2,16,128,128]{3,2,1,0:T(8,128)S(1)}, f32[2,16,128,128]{3,2,1,0:T(8,128)}, u32[]{:S(2)}) copy-start(f32[2,16,128,128]{3,2,1,0:T(8,128)} %get-tuple-element.185) | copy-start | bytes 6291460 | tf_op jit(solution)/shard_map/while/body/eval_jaxpr/cond
  281.7 1.3 copy-start.1
  322.5 9.6 %copy-start = (f32[2,16,128,128]{3,2,1,0:T(8,128)S(1)}, f32[2,16,128,128]{3,2,1,0:T(8,128)}, u32[]{:S(2)}) copy-start(f32[2,16,128,128]{3,2,1,0:T(8,128)} %get-tuple-element.185) | copy-start | bytes 6291460 | tf_op jit(solution)/shard_map/while/body/eval_jaxpr/cond
  334.8 1.3 copy-start.1
  339.8 16.6 %all-to-all-start.6 = ((bf16[128,32,128]{2,1,0:T(8,128)(2,1)}), bf16[128,32,128]{2,1,0:T(8,128)(2,1)S(1)}, u32[]{:S(2)}, u32[]{:S(2)}) async-start(bf16[128,32,128]{2,1,0:T(8,128)(2,1)} %bitcast.130), calls=%async_computation.6 | async-start | bytes 2097152 | tf_op jit(solution)/shard_map/all_to_all | solution.py:128
  356.4 51.8 %all-to-all-start.7 = ((bf16[128,32,4,128]{3,1,2,0:T(8,128)(2,1)}), bf16[128,32,4,128]{3,1,2,0:T(8,128)(2,1)}, u32[]{:S(2)}, u32[]{:S(2)}) async-start(bf16[128,32,4,128]{3,1,2,0:T(8,128)(2,1)} %bitcast.126), calls=%async_computation.7 | async-start | bytes 8388608 | tf_op jit(solution)/shard_map/all_to_all | solution.py:129
Sparse Core Ops, SparseCore 0:
  19.9 28.8 all-gather.2
  52.2 35.0 all-gather.4
where the time goes:
time: 426 us; the launch traced here: 424 us
  matrix products  185 us (43%)
  waiting for transfers between devices  67.5 us (16%)
  local copies, waits for them, and re-layouts  56.6 us (13%)
  blocking collectives  43.3 us (10%)
  starting transfers between devices  26.8 us (6%)
  other arithmetic  25.2 us (6%)
  between operations  14.2 us (3%)
  loops' own time  5.56 us (1%)
    dot_general x4, matrix products, update(): jnp.einsum('grpqd,kgd->grpqk', tangent_heads, key_block, preferred_elemen...  53 us
    all_to_all x1, waiting for transfers between devices, per_device(): lax.all_to_all(tangent_rows, 'uly', split_axis=0, concat_axis=1, tiled=True)  45.8 us
    dot_general x4, matrix products, update(): jnp.einsum('grpqk,kgd->grpqd', weighted.astype(jnp.bfloat16), value_block...  39.9 us
    dot_general x4, matrix products, update(): jnp.einsum('grqk,kgpd->grpqd', weights_half, value_tan, preferred_element...  38.2 us
    dot_general x4, matrix products, update(): jnp.einsum('grqd,kgpd->grpqk', query_heads, key_tan, preferred_element_ty...  36.5 us
    unnamed x9, local copies, waits for them, and re-layouts  21.2 us
    all_gather x1, blocking collectives, per_device(): key_piece = lax.all_gather(head_keys, 'blk', axis=0, tiled=True)  17.9 us
    all_gather x1, blocking collectives, per_device(): value_piece = lax.all_gather(head_values, 'blk', axis=0, tiled=True)  14.7 us
  transfers between devices with their start and end apart: 9, of which 7 were waited for; matrix products, arithmetic and copies ran while one was open for 9% of the time, Pallas kernels for 0%

commit v1 on v0

--- a/solution.py
+++ b/solution.py
@@ -126,7 +126,12 @@
     )
     attention_out, tangent_out = (
         lax.all_to_all(output_rows, "uly", split_axis=0, concat_axis=1, tiled=True),
-        lax.all_to_all(tangent_rows, "uly", split_axis=0, concat_axis=1, tiled=True),
+        jnp.concatenate(
+            lax.all_to_all(
+                jnp.stack(jnp.split(tangent_rows, lax.axis_size("uly"), axis=0)), "uly", 0, 0
+            ),
+            axis=1,
+        ),
     )
     return (attention_out, tangent_out)
 

time: 426 us -> 437 us (1.026)
  other arithmetic: 25.2 us -> 31.4 us
    another operation x0 -> x1, other arithmetic: none -> 6.34 us  [per_device(): jnp.stack(jnp.split(tangent_rows, lax.axis_size('uly'), axis=0))]
    split x0 -> x5, local copies, waits for them, and re-layouts: none -> 5.45 us  [per_device(): jnp.split(tangent_rows, lax.axis_size('uly'), axis=0)]
    transpose x1 -> x0, local copies, waits for them, and re-layouts: 4.71 us -> none  [per_device(): jnp.transpose(tangent.astype(jnp.bfloat16), (3, 0, 1, 2, 4))]
  transfers between devices with their start and end apart: 9 -> 9, of which waited for: 7 -> 7; matrix products, arithmetic and copies ran while one was open for 9% -> 8% of each run, Pallas kernels for 0% -> 0%
where the time goes in v1:
time: 437 us; the launch traced here: 435 us
  matrix products  185 us (42%)
  waiting for transfers between devices  71.4 us (16%)
  local copies, waits for them, and re-layouts  57.4 us (13%)
  blocking collectives  43.3 us (10%)
  other arithmetic  31.4 us (7%)
  starting transfers between devices  26.8 us (6%)
  between operations  14.3 us (3%)
  loops' own time  5.76 us (1%)
    dot_general x4, matrix products, update(): jnp.einsum('grpqd,kgd->grpqk', tangent_heads, key_block, preferred_elemen...  53 us
    all_to_all x1, waiting for transfers between devices, per_device(): lax.all_to_all(jnp.stack(jnp.split(tangent_rows, lax.axis_size('uly'), ax...  45.8 us
    dot_general x4, matrix products, update(): jnp.einsum('grpqk,kgd->grpqd', weighted.astype(jnp.bfloat16), value_block...  39.9 us
    dot_general x4, matrix products, update(): jnp.einsum('grqk,kgpd->grpqd', weights_half, value_tan, preferred_element...  38.2 us
    dot_general x4, matrix products, update(): jnp.einsum('grqd,kgpd->grpqk', query_heads, key_tan, preferred_element_ty...  36.5 us
    unnamed x9, local copies, waits for them, and re-layouts  21.2 us
    all_gather x1, blocking collectives, per_device(): key_piece = lax.all_gather(head_keys, 'blk', axis=0, tiled=True)  17.9 us
    all_gather x1, blocking collectives, per_device(): value_piece = lax.all_gather(head_values, 'blk', axis=0, tiled=True)  14.8 us
  transfers between devices with their start and end apart: 9, of which 7 were waited for; matrix products, arithmetic and copies ran while one was open for 8% of the time, Pallas kernels for 0%

profile of v1, /device:TPU:0, one launch (start us, length us, event | category | flops | bytes accessed | tf_op | source)
XLA Modules:
  0.0 435.5 jit_solution(14963489451604579169)
XLA Ops:
  8.3 10.7 %all_to_all.125 = bf16[32,8,4,128]{3,0,2,1:T(8,128)(2,1)S(1)} all-to-all(bf16[32,8,4,128]{3,0,2,1:T(8,128)(2,1)S(1)} %copy.120), channel_id=1, replica_groups=mesh['blk'=8,'uly'=4] {'uly'}, dimensions={1} | all-to-all | bytes 524288 | tf_op jit(solution)/shard_map/all_to_all | solution.py:94
  65.5 17.9 %all_gather.12 = bf16[1024,2,128]{2,0,1:T(8,128)(2,1)S(1)} all-gather(bf16[128,2,128]{2,0,1:T(8,128)(2,1)S(1)} %bitcast.144), channel_id=1, replica_groups=mesh['blk'=8,'uly'=4] {'blk'}, dimensions={0}, use_global_device_ids=true | all-gather | bytes 589824 | tf_op jit(solution)/shard_map/all_gather | solution.py:99
  84.3 14.8 %all_gather.13 = bf16[1024,2,128]{2,0,1:T(8,128)(2,1)S(1)} all-gather(bf16[128,2,128]{2,0,1:T(8,128)(2,1)S(1)} %bitcast.145), channel_id=1, replica_groups=mesh['blk'=8,'uly'=4] {'blk'}, dimensions={0}, use_global_device_ids=true | all-gather | bytes 589824 | tf_op jit(solution)/shard_map/all_gather | solution.py:101
  123.5 212.6 %while.18 = (s32[]{:T(128)}, f32[2,16,128]{2,1,0:T(8,128)S(1)}, f32[2,16,128]{2,1,0:T(8,128)S(1)}, f32[2,16,128,128]{3,2,1,0:T(8,128)}, f32[2,16,4,128,128]{4,3,...) while((s32[]{:T(128)}, f32[2,16,128]{2,1,0:T(8,128)S(1)}, ...), condition=%wide.region_10.11_spmd, body=%wide.region_3.10_spmd.sunk | while | flops 4875936256 | bytes 138631600 | solution.py:114
  125.7 51.2 %conditional.2 = ((f32[2,16,128]{2,1,0:T(8,128)S(1)}, f32[2,16,128]{2,1,0:T(8,128)S(1)}, f32[2,16,128,128]{3,2,1,0:T(8,128)}, f32[2,16,4,128,128]{4,3,2,1,0:T(8,128)}, f32[2,16,4,128]{3,2,1,0:T(4,128)S(1)})) conditional(s32[]{:T(128)} %convert_element_type.33, (f32[2,16,128]{2,1,0:T(8,128)S(1)}, f32[2,16,128]{2,1,0:T(8,128)S(1)}, ...), branch_computations={%region_5.5_spmd, %region_6.9_spmd} | conditional | flops 4875935744 | bytes 138629216 | solution.py:83
  130.8 9.1 %fusion.7 = f32[2,256,4,16,128]{4,1,2,3,0:T(8,128)} fusion(bf16[2,16,128,128]{3,2,1,0:T(8,128)(2,1)S(1)} %get-tuple-element.183, bf16[4,256,2,4,128]{4,1,3,2,0:T(8,128)(2,1)} %get-tuple-element.189, s32[]{:T(128)} %get-tuple-element.182), kind=kOutput, calls=%fused_computation.13 | convolution fusion | flops 1073741824 | bytes 18350592 | tf_op jit(solution)/shard_map/while/body/eval_jaxpr/cond/branch_1_fun/grqd,kgpd->grpqk/dot_general | solution.py:57
  139.9 13.3 %fusion.40 = (f32[2,16,4,128]{3,2,1,0:T(4,128)S(1)}, bf16[2,16,4,128,256]{3,4,2,1,0:T(8,128)(2,1)}) fusion(f32[2,16,128,256]{2,3,1,0:T(8,128)} %get-tuple-element.340, f32[2,256,4,16,128]{4,1,2,3,0:T(8,128)} %fusion.7, bf16[2,16,4,128,128]{4,3,2,1,0:T(8,128)(2,1)} %get-tuple-element.188, bf16[4,256,2,128]{3,1,2,0:T(8,128)(2,1)} %get-tuple-element.181, ...), kind=kOutput, calls=%fused_computation.71 | convolution fusion | flops 1090502656 | bytes 33751552 | tf_op jit(solution)/shard_map/while/body/eval_jaxpr/cond/branch_1_fun/grpqd,kgd->grpqk/dot_general | solution.py:54
  153.2 10.0 %fusion.1 = f32[2,16,4,128,128]{4,3,2,1,0:T(8,128)} fusion(bf16[2,16,4,128,256]{3,4,2,1,0:T(8,128)(2,1)} %get-tuple-element.345, bf16[4,256,2,128]{3,1,2,0:T(8,128)(2,1)} %get-tuple-element.186, s32[]{:T(128)} %get-tuple-element.182), kind=kOutput, calls=%fused_computation.3 | convolution fusion | flops 1073741824 | bytes 16908800 | tf_op jit(solution)/shard_map/while/body/eval_jaxpr/cond/branch_1_fun/grpqk,kgd->grpqd/dot_general | solution.py:67
  163.2 9.5 %bitcast_add_fusion.1 = f32[2,16,4,128,128]{4,3,2,1,0:T(8,128)} fusion(f32[2,16,4,128,128]{4,3,2,1,0:T(8,128)} %fusion.1, f32[2,16,4,128,128]{4,3,2,1,0:T(8,128)} %get-tuple-element.187, f32[2,16,128]{2,1,0:T(8,128)S(1)} %get-tuple-element.333, bf16[4,256,2,4,128]{4,1,3,2,0:T(8,128)(2,1)S(1)} %get-tuple-element.190, s32[]{:T(128)} %get-tuple-element.182, ...), kind=kOutput, calls=%fused_computation.2 | convolution fusion | flops 1085276160 | bytes 29949956 | tf_op jit(solution)/shard_map/while/body/eval_jaxpr/cond/branch_1_fun/grqk,kgpd->grpqd/dot_general | solution.py:73
  178.8 51.2 %conditional.2 = ((f32[2,16,128]{2,1,0:T(8,128)S(1)}, f32[2,16,128]{2,1,0:T(8,128)S(1)}, f32[2,16,128,128]{3,2,1,0:T(8,128)}, f32[2,16,4,128,128]{4,3,2,1,0:T(8,128)}, f32[2,16,4,128]{3,2,1,0:T(4,128)S(1)})) conditional(s32[]{:T(128)} %convert_element_type.33, (f32[2,16,128]{2,1,0:T(8,128)S(1)}, f32[2,16,128]{2,1,0:T(8,128)S(1)}, ...), branch_computations={%region_5.5_spmd, %region_6.9_spmd} | conditional | flops 4875935744 | bytes 138629216 | solution.py:83
  183.9 9.1 %fusion.7 = f32[2,256,4,16,128]{4,1,2,3,0:T(8,128)} fusion(bf16[2,16,128,128]{3,2,1,0:T(8,128)(2,1)S(1)} %get-tuple-element.183, bf16[4,256,2,4,128]{4,1,3,2,0:T(8,128)(2,1)} %get-tuple-element.189, s32[]{:T(128)} %get-tuple-element.182), kind=kOutput, calls=%fused_computation.13 | convolution fusion | flops 1073741824 | bytes 18350592 | tf_op jit(solution)/shard_map/while/body/eval_jaxpr/cond/branch_1_fun/grqd,kgpd->grpqk/dot_general | solution.py:57
  193.0 13.3 %fusion.40 = (f32[2,16,4,128]{3,2,1,0:T(4,128)S(1)}, bf16[2,16,4,128,256]{3,4,2,1,0:T(8,128)(2,1)}) fusion(f32[2,16,128,256]{2,3,1,0:T(8,128)} %get-tuple-element.340, f32[2,256,4,16,128]{4,1,2,3,0:T(8,128)} %fusion.7, bf16[2,16,4,128,128]{4,3,2,1,0:T(8,128)(2,1)} %get-tuple-element.188, bf16[4,256,2,128]{3,1,2,0:T(8,128)(2,1)} %get-tuple-element.181, ...), kind=kOutput, calls=%fused_computation.71 | convolution fusion | flops 1090502656 | bytes 33751552 | tf_op jit(solution)/shard_map/while/body/eval_jaxpr/cond/branch_1_fun/grpqd,kgd->grpqk/dot_general | solution.py:54
  206.3 10.0 %fusion.1 = f32[2,16,4,128,128]{4,3,2,1,0:T(8,128)} fusion(bf16[2,16,4,128,256]{3,4,2,1,0:T(8,128)(2,1)} %get-tuple-element.345, bf16[4,256,2,128]{3,1,2,0:T(8,128)(2,1)} %get-tuple-element.186, s32[]{:T(128)} %get-tuple-element.182), kind=kOutput, calls=%fused_computation.3 | convolution fusion | flops 1073741824 | bytes 16908800 | tf_op jit(solution)/shard_map/while/body/eval_jaxpr/cond/branch_1_fun/grpqk,kgd->grpqd/dot_general | solution.py:67
  216.3 9.5 %bitcast_add_fusion.1 = f32[2,16,4,128,128]{4,3,2,1,0:T(8,128)} fusion(f32[2,16,4,128,128]{4,3,2,1,0:T(8,128)} %fusion.1, f32[2,16,4,128,128]{4,3,2,1,0:T(8,128)} %get-tuple-element.187, f32[2,16,128]{2,1,0:T(8,128)S(1)} %get-tuple-element.333, bf16[4,256,2,4,128]{4,1,3,2,0:T(8,128)(2,1)S(1)} %get-tuple-element.190, s32[]{:T(128)} %get-tuple-element.182, ...), kind=kOutput, calls=%fused_computation.2 | convolution fusion | flops 1085276160 | bytes 29949956 | tf_op jit(solution)/shard_map/while/body/eval_jaxpr/cond/branch_1_fun/grqk,kgpd->grpqd/dot_general | solution.py:73
  231.9 51.2 %conditional.2 = ((f32[2,16,128]{2,1,0:T(8,128)S(1)}, f32[2,16,128]{2,1,0:T(8,128)S(1)}, f32[2,16,128,128]{3,2,1,0:T(8,128)}, f32[2,16,4,128,128]{4,3,2,1,0:T(8,128)}, f32[2,16,4,128]{3,2,1,0:T(4,128)S(1)})) conditional(s32[]{:T(128)} %convert_element_type.33, (f32[2,16,128]{2,1,0:T(8,128)S(1)}, f32[2,16,128]{2,1,0:T(8,128)S(1)}, ...), branch_computations={%region_5.5_spmd, %region_6.9_spmd} | conditional | flops 4875935744 | bytes 138629216 | solution.py:83
  237.0 9.1 %fusion.7 = f32[2,256,4,16,128]{4,1,2,3,0:T(8,128)} fusion(bf16[2,16,128,128]{3,2,1,0:T(8,128)(2,1)S(1)} %get-tuple-element.183, bf16[4,256,2,4,128]{4,1,3,2,0:T(8,128)(2,1)} %get-tuple-element.189, s32[]{:T(128)} %get-tuple-element.182), kind=kOutput, calls=%fused_computation.13 | convolution fusion | flops 1073741824 | bytes 18350592 | tf_op jit(solution)/shard_map/while/body/eval_jaxpr/cond/branch_1_fun/grqd,kgpd->grpqk/dot_general | solution.py:57
  246.1 13.3 %fusion.40 = (f32[2,16,4,128]{3,2,1,0:T(4,128)S(1)}, bf16[2,16,4,128,256]{3,4,2,1,0:T(8,128)(2,1)}) fusion(f32[2,16,128,256]{2,3,1,0:T(8,128)} %get-tuple-element.340, f32[2,256,4,16,128]{4,1,2,3,0:T(8,128)} %fusion.7, bf16[2,16,4,128,128]{4,3,2,1,0:T(8,128)(2,1)} %get-tuple-element.188, bf16[4,256,2,128]{3,1,2,0:T(8,128)(2,1)} %get-tuple-element.181, ...), kind=kOutput, calls=%fused_computation.71 | convolution fusion | flops 1090502656 | bytes 33751552 | tf_op jit(solution)/shard_map/while/body/eval_jaxpr/cond/branch_1_fun/grpqd,kgd->grpqk/dot_general | solution.py:54
  259.4 10.0 %fusion.1 = f32[2,16,4,128,128]{4,3,2,1,0:T(8,128)} fusion(bf16[2,16,4,128,256]{3,4,2,1,0:T(8,128)(2,1)} %get-tuple-element.345, bf16[4,256,2,128]{3,1,2,0:T(8,128)(2,1)} %get-tuple-element.186, s32[]{:T(128)} %get-tuple-element.182), kind=kOutput, calls=%fused_computation.3 | convolution fusion | flops 1073741824 | bytes 16908800 | tf_op jit(solution)/shard_map/while/body/eval_jaxpr/cond/branch_1_fun/grpqk,kgd->grpqd/dot_general | solution.py:67
  269.4 9.5 %bitcast_add_fusion.1 = f32[2,16,4,128,128]{4,3,2,1,0:T(8,128)} fusion(f32[2,16,4,128,128]{4,3,2,1,0:T(8,128)} %fusion.1, f32[2,16,4,128,128]{4,3,2,1,0:T(8,128)} %get-tuple-element.187, f32[2,16,128]{2,1,0:T(8,128)S(1)} %get-tuple-element.333, bf16[4,256,2,4,128]{4,1,3,2,0:T(8,128)(2,1)S(1)} %get-tuple-element.190, s32[]{:T(128)} %get-tuple-element.182, ...), kind=kOutput, calls=%fused_computation.2 | convolution fusion | flops 1085276160 | bytes 29949956 | tf_op jit(solution)/shard_map/while/body/eval_jaxpr/cond/branch_1_fun/grqk,kgpd->grpqd/dot_general | solution.py:73
  285.0 51.2 %conditional.2 = ((f32[2,16,128]{2,1,0:T(8,128)S(1)}, f32[2,16,128]{2,1,0:T(8,128)S(1)}, f32[2,16,128,128]{3,2,1,0:T(8,128)}, f32[2,16,4,128,128]{4,3,2,1,0:T(8,128)}, f32[2,16,4,128]{3,2,1,0:T(4,128)S(1)})) conditional(s32[]{:T(128)} %convert_element_type.33, (f32[2,16,128]{2,1,0:T(8,128)S(1)}, f32[2,16,128]{2,1,0:T(8,128)S(1)}, ...), branch_computations={%region_5.5_spmd, %region_6.9_spmd} | conditional | flops 4875935744 | bytes 138629216 | solution.py:83
  299.2 13.3 %fusion.40 = (f32[2,16,4,128]{3,2,1,0:T(4,128)S(1)}, bf16[2,16,4,128,256]{3,4,2,1,0:T(8,128)(2,1)}) fusion(f32[2,16,128,256]{2,3,1,0:T(8,128)} %get-tuple-element.340, f32[2,256,4,16,128]{4,1,2,3,0:T(8,128)} %fusion.7, bf16[2,16,4,128,128]{4,3,2,1,0:T(8,128)(2,1)} %get-tuple-element.188, bf16[4,256,2,128]{3,1,2,0:T(8,128)(2,1)} %get-tuple-element.181, ...), kind=kOutput, calls=%fused_computation.71 | convolution fusion | flops 1090502656 | bytes 33751552 | tf_op jit(solution)/shard_map/while/body/eval_jaxpr/cond/branch_1_fun/grpqd,kgd->grpqk/dot_general | solution.py:54
  312.5 10.0 %fusion.1 = f32[2,16,4,128,128]{4,3,2,1,0:T(8,128)} fusion(bf16[2,16,4,128,256]{3,4,2,1,0:T(8,128)(2,1)} %get-tuple-element.345, bf16[4,256,2,128]{3,1,2,0:T(8,128)(2,1)} %get-tuple-element.186, s32[]{:T(128)} %get-tuple-element.182), kind=kOutput, calls=%fused_computation.3 | convolution fusion | flops 1073741824 | bytes 16908800 | tf_op jit(solution)/shard_map/while/body/eval_jaxpr/cond/branch_1_fun/grpqk,kgd->grpqd/dot_general | solution.py:67
  322.5 9.5 %bitcast_add_fusion.1 = f32[2,16,4,128,128]{4,3,2,1,0:T(8,128)} fusion(f32[2,16,4,128,128]{4,3,2,1,0:T(8,128)} %fusion.1, f32[2,16,4,128,128]{4,3,2,1,0:T(8,128)} %get-tuple-element.187, f32[2,16,128]{2,1,0:T(8,128)S(1)} %get-tuple-element.333, bf16[4,256,2,4,128]{4,1,3,2,0:T(8,128)(2,1)S(1)} %get-tuple-element.190, s32[]{:T(128)} %get-tuple-element.182, ...), kind=kOutput, calls=%fused_computation.2 | convolution fusion | flops 1085276160 | bytes 29949956 | tf_op jit(solution)/shard_map/while/body/eval_jaxpr/cond/branch_1_fun/grqk,kgpd->grpqd/dot_general | solution.py:73
  373.5 45.8 %all-to-all-done.7 = bf16[4,32,32,4,128]{4,3,2,1,0:T(4,128)(2,1)} async-done(((bf16[4,32,32,4,128]{4,3,2,1,0:T(4,128)(2,1)}), bf16[4,32,32,4,128]{4,3,2,1,0:T(4,128)(2,1)}, u32[]{:S(2)}, u32[]{:S(2)}) %all-to-all-start.7) | async-done | bytes 4194336 | tf_op jit(solution)/shard_map/all_to_all | solution.py:130
  (116 shorter events, 167.8 us)
Async XLA Ops:
  7.2 105.6 %all-gather.3.cloned.1.call-start = ((), (), s32[]{:S(2)}) async-start(), calls=%async_computation.8 | async-start | bytes 2359296 | tf_op jit(solution)/shard_map/all_gather | solution.py:100
  21.2 8.1 %all-to-all-start = ((bf16[32,8,128]{2,0,1:T(8,128)(2,1)}), bf16[32,8,128]{2,0,1:T(8,128)(2,1)S(1)}, u32[]{:S(2)}, u32[]{:S(2)}) async-start(bf16[32,8,128]{2,0,1:T(8,128)(2,1)} %copy.112), calls=%async_computation | async-start | bytes 131072 | tf_op jit(solution)/shard_map/all_to_all | solution.py:93
  29.3 8.1 %all-to-all-start.2 = ((bf16[32,8,128]{2,0,1:T(8,128)(2,1)}), bf16[32,8,128]{2,0,1:T(8,128)(2,1)S(1)}, u32[]{:S(2)}, u32[]{:S(2)}) async-start(bf16[32,8,128]{2,0,1:T(8,128)(2,1)} %copy.116), calls=%async_computation.2 | async-start | bytes 131072 | tf_op jit(solution)/shard_map/all_to_all | solution.py:95
  37.4 8.8 %all-to-all-start.5 = ((bf16[32,8,4,128]{3,0,2,1:T(8,128)(2,1)}), bf16[32,8,4,128]{3,0,2,1:T(8,128)(2,1)S(1)}, u32[]{:S(2)}, u32[]{:S(2)}) async-start(bf16[32,8,4,128]{3,0,2,1:T(8,128)(2,1)} %copy.122), calls=%async_computation.5 | async-start | bytes 524288 | tf_op jit(solution)/shard_map/all_to_all | solution.py:96
  46.2 13.5 %all-to-all-start.1 = ((bf16[32,128,128]{2,0,1:T(8,128)(2,1)}), bf16[32,128,128]{2,0,1:T(8,128)(2,1)S(1)}, u32[]{:S(2)}, u32[]{:S(2)}) async-start(bf16[32,128,128]{2,0,1:T(8,128)(2,1)} %copy.114), calls=%async_computation.1 | async-start | bytes 2097152 | tf_op jit(solution)/shard_map/all_to_all | solution.py:21
  49.7 66.2 %all-gather.5.cloned.1.call-start = ((), (), s32[]{:S(2)}) async-start(), calls=%async_computation.9 | async-start | bytes 2359296 | tf_op jit(solution)/shard_map/all_gather | solution.py:102
  57.1 7.5 %copy-start.2 = (s32[16]{0:T(128)S(1)}, s32[16]{0:T(128)}, u32[]{:S(2)}) copy-start(s32[16]{0:T(128)} %param.17) | copy-start | bytes 196
  59.7 47.7 %all-to-all-start.3 = ((bf16[32,128,4,128]{3,2,0,1:T(4,128)(2,1)}), bf16[32,128,4,128]{3,2,0,1:T(4,128)(2,1)}, u32[]{:S(2)}, u32[]{:S(2)}) async-start(bf16[32,128,4,128]{3,2,0,1:T(4,128)(2,1)} %copy.118), calls=%async_computation.3 | async-start | bytes 8388608 | tf_op jit(solution)/shard_map/all_to_all | solution.py:22
  163.1 9.6 %copy-start = (f32[2,16,128,128]{3,2,1,0:T(8,128)S(1)}, f32[2,16,128,128]{3,2,1,0:T(8,128)}, u32[]{:S(2)}) copy-start(f32[2,16,128,128]{3,2,1,0:T(8,128)} %get-tuple-element.185) | copy-start | bytes 6291460 | tf_op jit(solution)/shard_map/while/body/eval_jaxpr/cond
  175.5 1.3 copy-start.1
  216.3 9.6 %copy-start = (f32[2,16,128,128]{3,2,1,0:T(8,128)S(1)}, f32[2,16,128,128]{3,2,1,0:T(8,128)}, u32[]{:S(2)}) copy-start(f32[2,16,128,128]{3,2,1,0:T(8,128)} %get-tuple-element.185) | copy-start | bytes 6291460 | tf_op jit(solution)/shard_map/while/body/eval_jaxpr/cond
  228.6 1.3 copy-start.1
  269.4 9.6 %copy-start = (f32[2,16,128,128]{3,2,1,0:T(8,128)S(1)}, f32[2,16,128,128]{3,2,1,0:T(8,128)}, u32[]{:S(2)}) copy-start(f32[2,16,128,128]{3,2,1,0:T(8,128)} %get-tuple-element.185) | copy-start | bytes 6291460 | tf_op jit(solution)/shard_map/while/body/eval_jaxpr/cond
  281.7 1.3 copy-start.1
  322.5 9.6 %copy-start = (f32[2,16,128,128]{3,2,1,0:T(8,128)S(1)}, f32[2,16,128,128]{3,2,1,0:T(8,128)}, u32[]{:S(2)}) copy-start(f32[2,16,128,128]{3,2,1,0:T(8,128)} %get-tuple-element.185) | copy-start | bytes 6291460 | tf_op jit(solution)/shard_map/while/body/eval_jaxpr/cond
  334.8 1.3 copy-start.1
  350.9 16.6 %all-to-all-start.6 = ((bf16[128,32,128]{2,1,0:T(8,128)(2,1)}), bf16[128,32,128]{2,1,0:T(8,128)(2,1)S(1)}, u32[]{:S(2)}, u32[]{:S(2)}) async-start(bf16[128,32,128]{2,1,0:T(8,128)(2,1)} %bitcast.49), calls=%async_computation.6 | async-start | bytes 2097152 | tf_op jit(solution)/shard_map/all_to_all | solution.py:128
  367.6 51.8 %all-to-all-start.7 = ((bf16[4,32,32,4,128]{4,3,2,1,0:T(4,128)(2,1)}), bf16[4,32,32,4,128]{4,3,2,1,0:T(4,128)(2,1)}, u32[]{:S(2)}, u32[]{:S(2)}) async-start(bf16[4,32,32,4,128]{4,3,2,1,0:T(4,128)(2,1)} %pad_maximum_fusion), calls=%async_computation.7 | async-start | bytes 8388608 | tf_op jit(solution)/shard_map/all_to_all | solution.py:130
Sparse Core Ops, SparseCore 0:
  19.9 28.8 all-gather.2
  52.1 35.0 all-gather.4
